TPU v7x, 128 devices: a whole 4x4x4 slice. The times are simulated.
128 devices in a mesh: req: 16 (over y, z), mlp: 8 (over x, core).
Axes of the slice: x: 4, y: 4, z: 4, core: 2. Of those that a mesh axis runs over, the one named last changes fastest.
Arguments:
- queries: bfloat16 [2048, 5120], P('req', 'mlp'), may hold values from -6 to 6
- leaf_keys: bfloat16 [2048, 1024], P('req', 'mlp'), may hold values from -6 to 6
- leaf_token_values: bfloat16 [2048, 1024], P('req', 'mlp'), may hold values from -6 to 6
- key_value_pages: bfloat16 [512, 64, 2, 1024], P('req', None, None, 'mlp'), may hold values from -6 to 6
- page_holder: int32 [16, 6, 4], replicated, may hold values from 0 to 15, as said below
- page_slot: int32 [16, 6, 4], replicated, may hold values from 0 to 31
- segment_ids: int32 [2048], P('req'), may hold values from 0 to 7, as said below
- req_parent: int32 [16, 8], P('req'), may hold values from 0 to 3
- mid_parent: int32 [16, 4], P('req'), may hold values from 0 to 1
- node_len: int32 [16, 6], P('req'), may hold values from 1 to 256
- residual: bfloat16 [2048, 5120], P('req'), may hold values from -6 to 6
- out_proj: bfloat16 [5120, 5120], P('mlp'), may hold values from -0.078125 to 0.078125
- norm_gain: float32 [5120], replicated, may hold values from 0.5 to 1.5
- gate_proj: bfloat16 [5120, 13824], P(None, ('req', 'mlp')), may hold values from -0.078125 to 0.078125
- up_proj: bfloat16 [5120, 13824], P(None, ('req', 'mlp')), may hold values from -0.078125 to 0.078125
- down_proj: bfloat16 [13824, 5120], P(('req', 'mlp')), may hold values from -0.0546875 to 0.0546875
- next_gain: float32 [5120], replicated, may hold values from 0.5 to 1.5
- qkv_proj: bfloat16 [5120, 7168], P(None, 'mlp'), may hold values from -0.078125 to 0.078125
- qkv_bias: float32 [7168], P('mlp'), may hold values from -3 to 3
Outputs:
- layer_out: bfloat16 [2048, 5120], P(('req', 'mlp'))
- qkv_out: bfloat16 [2048, 7168], P('req', 'mlp')
Inputs may be any that keep to these rules, and one draw needn't show every extreme that they name: `segment_ids`: within each block of 128 tokens of one group the ids never fall, start at 0, and every id 0 to 7 occurs. `page_holder`: in each row (one group's prefix pages) exactly half of the entries name the row's own group; the other entries name other groups, no group more than 1 times in a row, and some group exactly 1 times.
All inputs are finite; a program needn't handle non-finite values.
Results may differ from a plain program's by a relative error of at most 0.02.
Values may be sent and summed in bfloat16 or wider, within the bound.
A program may use at most 192 MiB of HBM per device.

v0:
```python
import math
import jax
import jax.numpy as jnp
from jax import lax
from jax.sharding import PartitionSpec as P

HEAD_SIZE = 128
QUERY_PER_KV = 5
REQ_DEV = 8
ROOT_DEV = 2
MID_DEV = 4
NODES_DEV = 6
NODE_MAX = 256
EPS = 1e-06


def rms_norm(stream, gain):
    values = stream.astype(jnp.float32)
    mean_sq = jnp.mean(values * values, axis=-1, keepdims=True)
    return (values * lax.rsqrt(mean_sq + EPS) * gain).astype(jnp.bfloat16)


def attend(
    queries,
    leaf_keys,
    leaf_token_values,
    prefix_keys,
    prefix_values,
    segments,
    parents,
    roots,
    lengths,
):
    tokens = queries.shape[0]
    heads_kv = leaf_keys.shape[1] // HEAD_SIZE
    query_rows = queries.reshape(tokens, heads_kv, QUERY_PER_KV, HEAD_SIZE)
    keys = jnp.concatenate(
        [
            prefix_keys.reshape(-1, heads_kv, HEAD_SIZE),
            leaf_keys.reshape(tokens, heads_kv, HEAD_SIZE),
        ],
        0,
    )
    values = jnp.concatenate(
        [
            prefix_values.reshape(-1, heads_kv, HEAD_SIZE),
            leaf_token_values.reshape(tokens, heads_kv, HEAD_SIZE),
        ],
        0,
    )
    middle = jnp.sum((segments[:, None] == jnp.arange(REQ_DEV)[None, :]) * parents[None, :], axis=1)
    root = jnp.sum((middle[:, None] == jnp.arange(MID_DEV)[None, :]) * roots[None, :], axis=1)
    node = jnp.arange(NODES_DEV * NODE_MAX) // NODE_MAX
    inside = (jnp.arange(NODE_MAX)[None, :] < lengths[:, None]).reshape(-1)
    prefix_mask = (
        (node[None, :] == root[:, None]) | (node[None, :] == ROOT_DEV + middle[:, None])
    ) & inside[None, :]
    place = jnp.arange(tokens)
    leaf_mask = (segments[None, :] == segments[:, None]) & (place[None, :] <= place[:, None])
    mask = jnp.concatenate([prefix_mask, leaf_mask], 1)
    score = jnp.einsum(
        "tkgd,skd->tkgs", query_rows, keys, preferred_element_type=jnp.float32
    ) / math.sqrt(HEAD_SIZE)
    score = jnp.where(mask[:, None, None, :], score, -1e30)
    top = jnp.max(score, axis=-1, keepdims=True)
    expo = jnp.where(mask[:, None, None, :], jnp.exp(score - top), 0.0)
    total = jnp.sum(expo, axis=-1, keepdims=True)
    weights = expo.astype(jnp.bfloat16)
    summed = jnp.einsum("tkgs,skd->tkgd", weights, values, preferred_element_type=jnp.float32)
    return (summed / total).astype(jnp.bfloat16).reshape(tokens, -1)


def fetch_prefix(key_value_pages, page_holder, page_slot):
    groups = lax.axis_size("req")
    myself = lax.axis_index("req")
    holders = page_holder.reshape(groups, -1)
    slots = page_slot.reshape(groups, -1)
    token_count = holders.shape[1]
    room = (token_count // 2 + groups - 2) // (groups - 1)
    earlier = jnp.arange(token_count)[None, :] < jnp.arange(token_count)[:, None]
    same = holders[:, :, None] == holders[:, None, :]
    rank = jnp.sum(same & earlier[None, :, :], axis=-1)
    asked = (holders == myself) & (jnp.arange(groups)[:, None] != myself)
    picked = asked[:, None, :] & (rank[:, None, :] == jnp.arange(room)[None, :, None])
    send_slot = jnp.sum(jnp.where(picked, slots[:, None, :], 0), axis=-1)
    outgoing = key_value_pages[send_slot]
    incoming = lax.all_to_all(outgoing, "req", split_axis=0, concat_axis=0, tiled=True)
    flat_in = incoming.reshape((groups * room,) + incoming.shape[2:])
    own_holders = lax.dynamic_index_in_dim(holders, myself, 0, keepdims=False)
    own_slots = lax.dynamic_index_in_dim(slots, myself, 0, keepdims=False)
    own_rank = lax.dynamic_index_in_dim(rank, myself, 0, keepdims=False)
    remote = flat_in[own_holders * room + jnp.minimum(own_rank, room - 1)]
    local = key_value_pages[own_slots]
    pages = jnp.where((own_holders == myself)[:, None, None, None], local, remote)
    return pages.reshape(NODES_DEV * NODE_MAX, 2, -1)


def body(
    queries,
    leaf_keys,
    leaf_token_values,
    key_value_pages,
    page_holder,
    page_slot,
    segment_ids,
    req_parent,
    mid_parent,
    node_len,
    residual,
    out_proj,
    norm_gain,
    gate_proj,
    up_proj,
    down_proj,
    next_gain,
    qkv_proj,
    qkv_bias,
):
    prefix = fetch_prefix(key_value_pages, page_holder, page_slot)
    attention = attend(
        queries,
        leaf_keys,
        leaf_token_values,
        prefix[:, 0],
        prefix[:, 1],
        segment_ids,
        req_parent[0],
        mid_parent[0],
        node_len[0],
    )
    projected = jnp.dot(attention, out_proj, preferred_element_type=jnp.float32)
    group_tokens = queries.shape[0]
    groups = lax.axis_size("req")
    members = lax.axis_size("mlp")
    rows_mlp = group_tokens // members
    first_row = lax.axis_index("mlp") * rows_mlp
    head_part = lax.psum_scatter(
        projected.astype(jnp.bfloat16), "mlp", scatter_dimension=0, tiled=True
    ).astype(jnp.float32)
    own_resid = lax.dynamic_slice_in_dim(residual, first_row, rows_mlp, 0)
    stream = (own_resid.astype(jnp.float32) + head_part).astype(jnp.bfloat16)
    normed = rms_norm(stream, norm_gain)
    piece = lax.all_gather(normed, ("req", "mlp"), axis=0, tiled=True)
    gate = jnp.dot(piece, gate_proj, preferred_element_type=jnp.float32)
    upper = jnp.dot(piece, up_proj, preferred_element_type=jnp.float32)
    hidden_all = (jax.nn.silu(gate) * upper).astype(jnp.bfloat16)
    blocks = hidden_all.reshape(groups, members, rows_mlp, -1)
    regrouped = lax.all_to_all(blocks, "mlp", split_axis=1, concat_axis=3, tiled=True)
    hidden = regrouped.reshape(groups * rows_mlp, -1)
    mixed_all = jnp.dot(
        hidden,
        lax.all_gather(down_proj, "mlp", axis=0, tiled=True),
        preferred_element_type=jnp.float32,
    )
    mixed = lax.psum_scatter(
        mixed_all.astype(jnp.bfloat16), "req", scatter_dimension=0, tiled=True
    ).astype(jnp.float32)
    layer_out = (stream.astype(jnp.float32) + mixed).astype(jnp.bfloat16)
    next_rows = rms_norm(layer_out, next_gain)
    next_normed = lax.all_gather(next_rows, "mlp", axis=0, tiled=True)
    qkv_out = (
        jnp.dot(next_normed, qkv_proj, preferred_element_type=jnp.float32) + qkv_bias
    ).astype(jnp.bfloat16)
    return (layer_out, qkv_out)


def solution(mesh):
    placed = (
        P("req", "mlp"),
        P("req", "mlp"),
        P("req", "mlp"),
        P("req", None, None, "mlp"),
        P(),
        P(),
        P("req"),
        P("req", None),
        P("req", None),
        P("req", None),
        P("req", None),
        P("mlp", None),
        P(),
        P(None, ("req", "mlp")),
        P(None, ("req", "mlp")),
        P(("req", "mlp"), None),
        P(),
        P(None, "mlp"),
        P("mlp"),
    )
    return jax.shard_map(
        body,
        mesh=mesh,
        in_specs=placed,
        out_specs=(P(("req", "mlp"), None), P("req", "mlp")),
        check_vma=False,
    )
```

profile of v0, /device:TPU:1, one launch (start us, length us, event | category | flops | bytes accessed | tf_op | source)
XLA Modules:
  0.0 356.3 jit_solution(15968638742785638937)
XLA Ops:
  7.2 0.9 copy.70
  8.7 0.8 select_reduce_fusion
  9.5 3.6 %gather_fusion.1 = bf16[16,64,2,128]{3,2,1,0:T(2,128)(2,1)} fusion(bf16[32,64,2,128]{3,2,1,0:T(2,128)(2,1)} %param.22, s32[1024]{0:T(1024)S(1)} %pad_clamp_fusion.1), kind=kCustom, calls=%fused_computation.1 | custom fusion | bytes 1048640 | tf_op jit(solution)/shard_map/gather | solution.py:86
  13.1 8.6 %all-to-all-start = ((bf16[16,1,64,2,128]{4,3,2,1,0:T(2,128)(2,1)}), bf16[16,1,64,2,128]{4,3,2,1,0:T(2,128)(2,1)S(1)}, u32[]{:S(2)}, u32[]{:S(2)}) async-start(bf16[16,1,64,2,128]{4,3,2,1,0:T(2,128)(2,1)} %bitcast.9), calls=%async_computation | async-start | bytes 1048576 | tf_op jit(solution)/shard_map/all_to_all | solution.py:87
  21.8 0.8 constant_dynamic-slice_fusion.1
  22.6 0.8 select_reduce_fusion.1
  24.9 1.7 or_and_fusion
  26.8 3.4 gather_fusion
  30.4 0.8 copy.77
  31.3 0.9 pad_add_fusion
  32.2 2.1 gather_fusion.2
  35.3 0.8 fusion
  36.1 1.0 fusion.1
  37.2 1.3 fusion.15
  38.4 1.0 slice-done.1
  39.5 2.3 convolution_convert_fusion.1
  41.9 31.3 %reduce-scatter.3.cloned.1.call-done = bf16[16,5120]{1,0:T(8,128)(2,1)} async-done(((bf16[128,5120]{1,0:T(8,128)(2,1)}), bf16[16,5120]{1,0:T(8,128)(2,1)}) %reduce-scatter.3.cloned.1.call-update) | async-done | bytes 163856 | tf_op jit(solution)/shard_map/reduce_scatter | solution.py:137
  73.2 1.2 fusion.26
  74.4 0.8 fusion.28
  75.9 90.1 %all-gather.5.cloned.1.call-done = bf16[2048,5120]{1,0:T(8,128)(2,1)} async-done(((bf16[16,5120]{1,0:T(8,128)(2,1)}), bf16[2048,5120]{1,0:T(8,128)(2,1)}) %all-gather.5.cloned.1.call-update) | async-done | bytes 20971536 | tf_op jit(solution)/shard_map/all_gather | solution.py:143
  166.1 13.8 %fusion.46 = f32[2048,108]{0,1:T(8,128)S(1)} fusion(bf16[2048,5120]{1,0:T(8,128)(2,1)} %all-gather.5.cloned.1.call-done, bf16[5120,108]{0,1:T(8,128)(2,1)S(1)} %copy-done), kind=kOutput, calls=%fused_computation.86 | convolution fusion | flops 2264924160 | bytes 22962176 | tf_op jit(solution)/shard_map/dot_general | solution.py:144
  180.5 6.8 %fusion.3 = bf16[2048,108]{0,1:T(8,128)(2,1)S(1)} fusion(bf16[2048,5120]{1,0:T(8,128)(2,1)S(1)} %copy-done.9, bf16[5120,108]{0,1:T(8,128)(2,1)S(1)} %copy-done.10, f32[2048,108]{0,1:T(8,128)S(1)} %fusion.46), kind=kOutput, calls=%fused_computation.11 | convolution fusion | flops 2266251264 | bytes 23404544 | tf_op jit(solution)/shard_map/dot_general | solution.py:145
  187.5 0.9 copy.82
  188.4 4.3 %all-to-all-start.1 = ((bf16[16,8,16,108]{3,2,0,1:T(8,128)(2,1)}), bf16[16,8,16,108]{3,2,0,1:T(8,128)(2,1)S(1)}, u32[]{:S(2)}, u32[]{:S(2)}) async-start(bf16[16,8,16,108]{3,2,0,1:T(8,128)(2,1)} %copy.82), calls=%async_computation.2 | async-start | bytes 1048576 | tf_op jit(solution)/shard_map/all_to_all | solution.py:148
  192.7 33.1 %all-gather.9.cloned.1.call-done = bf16[8,108,5120]{2,1,0:T(8,128)(2,1)} async-done(((bf16[1,108,5120]{2,1,0:T(8,128)(2,1)}), bf16[8,108,5120]{2,1,0:T(8,128)(2,1)}) %all-gather.9.cloned.1.call-update) | async-done | bytes 8847376 | tf_op jit(solution)/shard_map/all_gather | solution.py:152
  225.8 8.0 %reshape.279 = bf16[864,5120]{1,0:T(8,128)(2,1)} reshape(bf16[8,108,5120]{2,1,0:T(8,128)(2,1)} %all-gather.9.cloned.1.call-done) | data formatting | bytes 17694720
  234.6 7.7 %convolution_convert_fusion = bf16[256,5120]{1,0:T(8,128)(2,1)} fusion(bf16[256,864]{1,0:T(8,128)(2,1)S(1)} %reshape.253, bf16[864,5120]{1,0:T(8,128)(2,1)} %reshape.279), kind=kOutput, calls=%fused_computation.3 | convolution fusion | flops 2266234880 | bytes 11911168 | tf_op jit(solution)/shard_map/dot_general | solution.py:150
  242.3 73.7 %reduce-scatter.5.cloned.1.call-done = bf16[16,5120]{1,0:T(8,128)(2,1)} async-done(((bf16[256,5120]{1,0:T(8,128)(2,1)}), bf16[16,5120]{1,0:T(8,128)(2,1)}) %reduce-scatter.5.cloned.1.call-update) | async-done | bytes 163856 | tf_op jit(solution)/shard_map/reduce_scatter | solution.py:155
  316.1 1.1 fusion.23
  317.2 0.8 fusion.25
  318.0 25.4 %all-gather.7.cloned.1.call-done = bf16[128,5120]{1,0:T(8,128)(2,1)} async-done(((bf16[16,5120]{1,0:T(8,128)(2,1)}), bf16[128,5120]{1,0:T(8,128)(2,1)}) %all-gather.7.cloned.1.call-update) | async-done | bytes 1310736 | tf_op jit(solution)/shard_map/all_gather | solution.py:160
  343.4 6.3 %fusion.8 = bf16[128,896]{1,0:T(8,128)(2,1)} fusion(bf16[128,5120]{1,0:T(8,128)(2,1)} %all-gather.7.cloned.1.call-done, bf16[5120,896]{1,0:T(8,128)(2,1)} %param.36, f32[896]{0:T(1024)S(1)} %copy-done.7), kind=kOutput, calls=%fused_computation.16 | convolution fusion | flops 1174634496 | bytes 10718720 | tf_op jit(solution)/shard_map/dot_general | solution.py:162
  (72 shorter events, 6.2 us)
Async XLA Ops:
  7.2 158.9 %copy-start = (bf16[5120,108]{0,1:T(8,128)(2,1)S(1)}, bf16[5120,108]{0,1:T(8,128)(2,1)}, u32[]{:S(2)}) copy-start(bf16[5120,108]{0,1:T(8,128)(2,1)} %param.32) | copy-start | bytes 3317764
  7.2 24.0 %copy-start.8 = (s32[128]{0:T(128)S(1)}, s32[128]{0:T(128)}, u32[]{:S(2)}) copy-start(s32[128]{0:T(128)} %param.25) | copy-start | bytes 1540
  7.2 23.2 %copy-start.3 = (bf16[128,640]{1,0:T(8,128)(2,1)S(1)}, bf16[128,640]{1,0:T(8,128)(2,1)}, u32[]{:S(2)}) copy-start(bf16[128,640]{1,0:T(8,128)(2,1)} %param.19) | copy-start | bytes 491524
  13.1 19.2 %all-to-all-start = ((bf16[16,1,64,2,128]{4,3,2,1,0:T(2,128)(2,1)}), bf16[16,1,64,2,128]{4,3,2,1,0:T(2,128)(2,1)S(1)}, u32[]{:S(2)}, u32[]{:S(2)}) async-start(bf16[16,1,64,2,128]{4,3,2,1,0:T(2,128)(2,1)} %bitcast.9), calls=%async_computation | async-start | bytes 1048576 | tf_op jit(solution)/shard_map/all_to_all | solution.py:87
  21.7 51.5 %reduce-scatter.3.cloned.1.call-start = ((), (), s32[]{:S(2)}) async-start(), calls=%async_computation.4 | async-start | bytes 1474560 | tf_op jit(solution)/shard_map/reduce_scatter | solution.py:137
  30.4 4.6 %copy-start.11 = (bf16[128,128]{1,0:T(8,128)(2,1)S(1)}, bf16[128,128]{1,0:T(8,128)(2,1)}, u32[]{:S(2)}) copy-start(bf16[128,128]{1,0:T(8,128)(2,1)} %param.20) | copy-start | bytes 98308
  34.4 0.9 copy-start.4
  35.3 1.9 copy-start.12
  36.1 2.4 slice-start
  37.1 2.3 slice-start.1
  39.5 34.9 %copy-start.5 = (f32[5120]{0:T(1024)S(1)}, f32[5120]{0:T(1024)}, u32[]{:S(2)}) copy-start(f32[5120]{0:T(1024)} %param.31) | copy-start | bytes 61444
  41.9 124.2 %all-gather.5.cloned.1.call-start = ((), (), s32[]{:S(2)}) async-start(), calls=%async_computation.5 | async-start | bytes 21135360 | tf_op jit(solution)/shard_map/all_gather | solution.py:143
  75.2 150.6 %all-gather.9.cloned.1.call-start = ((), (), s32[]{:S(2)}) async-start(), calls=%async_computation.8 | async-start | bytes 10321920 | tf_op jit(solution)/shard_map/all_gather | solution.py:152
  75.9 104.0 %copy-start.10 = (bf16[5120,108]{0,1:T(8,128)(2,1)S(1)}, bf16[5120,108]{0,1:T(8,128)(2,1)}, u32[]{:S(2)}) copy-start(bf16[5120,108]{0,1:T(8,128)(2,1)} %param.33) | copy-start | bytes 3317764
  166.1 14.4 %copy-start.9 = (bf16[2048,5120]{1,0:T(8,128)(2,1)S(1)}, bf16[2048,5120]{1,0:T(8,128)(2,1)}, u32[]{:S(2)}) copy-start(bf16[2048,5120]{1,0:T(8,128)(2,1)} %all-gather.5.cloned.1.call-done) | copy-start | bytes 62914564
  188.4 45.4 %all-to-all-start.1 = ((bf16[16,8,16,108]{3,2,0,1:T(8,128)(2,1)}), bf16[16,8,16,108]{3,2,0,1:T(8,128)(2,1)S(1)}, u32[]{:S(2)}, u32[]{:S(2)}) async-start(bf16[16,8,16,108]{3,2,0,1:T(8,128)(2,1)} %copy.82), calls=%async_computation.2 | async-start | bytes 1048576 | tf_op jit(solution)/shard_map/all_to_all | solution.py:148
  192.7 123.4 %reduce-scatter.5.cloned.1.call-start = ((), (), s32[]{:S(2)}) async-start(), calls=%async_computation.6 | async-start | bytes 2785280 | tf_op jit(solution)/shard_map/reduce_scatter | solution.py:155
  234.6 82.6 %copy-start.6 = (f32[5120]{0:T(1024)S(1)}, f32[5120]{0:T(1024)}, u32[]{:S(2)}) copy-start(f32[5120]{0:T(1024)} %param.35) | copy-start | bytes 61444
  234.6 108.8 %copy-start.7 = (f32[896]{0:T(1024)S(1)}, f32[896]{0:T(1024)}, u32[]{:S(2)}) copy-start(f32[896]{0:T(1024)} %param.37) | copy-start | bytes 10756
  242.3 101.1 %all-gather.7.cloned.1.call-start = ((), (), s32[]{:S(2)}) async-start(), calls=%async_computation.7 | async-start | bytes 1474560 | tf_op jit(solution)/shard_map/all_gather | solution.py:160
  317.1 32.6 %copy-start.2 = (bf16[16,5120]{1,0:T(8,128)(2,1)}, bf16[16,5120]{1,0:T(8,128)(2,1)S(1)}, u32[]{:S(2)}) copy-start(bf16[16,5120]{1,0:T(8,128)(2,1)S(1)} %get-tuple-element.3) | copy-start | bytes 491524
  343.4 6.3 %copy-start.1 = (bf16[5120,108]{0,1:T(8,128)(2,1)S(1)}, bf16[5120,108]{0,1:T(8,128)(2,1)}, u32[]{:S(2)}) copy-start(bf16[5120,108]{0,1:T(8,128)(2,1)} %param.32) | copy-start | bytes 3317764
Sparse Core Ops, SparseCore 0:
  42.0 31.1 reduce-scatter.2
  76.8 89.2 all-gather.4
  167.8 58.0 all-gather.8
  242.4 73.6 reduce-scatter.4
  318.2 25.1 all-gather.6
where the time goes:
time: 357 us; the launch traced here: 356 us
  waiting for transfers between devices  254 us (71%)
  matrix products  39 us (11%)
  local copies, waits for them, and re-layouts  24.3 us (7%)
  between operations  14.1 us (4%)
  starting transfers between devices  13.2 us (4%)
  other arithmetic  11.4 us (3%)
    all_gather x1, waiting for transfers between devices, body(): piece = lax.all_gather(normed, ('req', 'mlp'), axis=0, tiled=True)  90.1 us
    reduce_scatter x1, waiting for transfers between devices, body(): lax.psum_scatter(mixed_all.astype(jnp.bfloat16), 'req', scatter_dimension...  73.7 us
    all_gather x1, waiting for transfers between devices, body(): lax.all_gather(down_proj, 'mlp', axis=0, tiled=True)  33.1 us
    reduce_scatter x1, waiting for transfers between devices, body(): lax.psum_scatter(projected.astype(jnp.bfloat16), 'mlp', scatter_dimension...  31.3 us
    all_gather x1, waiting for transfers between devices, body(): next_normed = lax.all_gather(next_rows, 'mlp', axis=0, tiled=True)  25.4 us
    dot_general x1, matrix products, body(): gate = jnp.dot(piece, gate_proj, preferred_element_type=jnp.float32)  13.8 us
    unnamed x33, local copies, waits for them, and re-layouts  10.9 us
    all_to_all x1, starting transfers between devices, fetch_prefix(): lax.all_to_all(outgoing, 'req', split_axis=0, concat_axis=0, tiled=True)  8.6 us
  transfers between devices with their start and end apart: 7, of which 5 were waited for; matrix products, arithmetic and copies ran while one was open for 11% of the time, Pallas kernels for 0%

commit v1 on v0

--- a/solution.py
+++ b/solution.py
@@ -140,7 +140,10 @@
     own_resid = lax.dynamic_slice_in_dim(residual, first_row, rows_mlp, 0)
     stream = (own_resid.astype(jnp.float32) + head_part).astype(jnp.bfloat16)
     normed = rms_norm(stream, norm_gain)
-    piece = lax.all_gather(normed, ("req", "mlp"), axis=0, tiled=True)
+    piece = jnp.concatenate(
+        lax.all_to_all(jnp.stack([normed] * lax.axis_size(("req", "mlp"))), ("req", "mlp"), 0, 0),
+        axis=0,
+    )
     gate = jnp.dot(piece, gate_proj, preferred_element_type=jnp.float32)
     upper = jnp.dot(piece, up_proj, preferred_element_type=jnp.float32)
     hidden_all = (jax.nn.silu(gate) * upper).astype(jnp.bfloat16)

time: 357 us -> 588 us (1.65)
  waiting for transfers between devices: 254 us -> 452 us
  starting transfers between devices: 13.2 us -> 36.1 us
  local copies, waits for them, and re-layouts: 24.3 us -> 31.2 us
    all_to_all x0 -> x1, waiting for transfers between devices: none -> 319 us  [body(): lax.all_to_all(jnp.stack([normed] * lax.axis_size(('req', 'mlp'))), ('req...]
    all_gather x1 -> x0, waiting for transfers between devices: 90.1 us -> none  [body(): piece = lax.all_gather(normed, ('req', 'mlp'), axis=0, tiled=True)]
    all_gather x1, waiting for transfers between devices: 33.1 us -> 0.01 us  [body(): lax.all_gather(down_proj, 'mlp', axis=0, tiled=True)]
    all_to_all x1, starting transfers between devices: 4.27 us -> 16.8 us  [body(): lax.all_to_all(blocks, 'mlp', split_axis=1, concat_axis=3, tiled=True)]
    all_to_all x0 -> x1, starting transfers between devices: none -> 10.3 us  [body(): lax.all_to_all(jnp.stack([normed] * lax.axis_size(('req', 'mlp'))), ('req...]
    another operation x0 -> x1, local copies, waits for them, and re-layouts: none -> 7.56 us  [body(): jnp.stack([normed] * lax.axis_size(('req', 'mlp')))]
    dot_general x1, matrix products: 6.76 us -> 13.8 us  [body(): upper = jnp.dot(piece, up_proj, preferred_element_type=jnp.float32)]
  transfers between devices with their start and end apart: 7 -> 7, of which waited for: 5 -> 5; matrix products, arithmetic and copies ran while one was open for 11% -> 8% of each run, Pallas kernels for 0% -> 0%
where the time goes in v1:
time: 588 us; the launch traced here: 587 us
  waiting for transfers between devices  452 us (77%)
  matrix products  43.2 us (7%)
  starting transfers between devices  36.1 us (6%)
  local copies, waits for them, and re-layouts  31.2 us (5%)
  between operations  14.1 us (2%)
  other arithmetic  10.8 us (2%)
    all_to_all x1, waiting for transfers between devices, body(): lax.all_to_all(jnp.stack([normed] * lax.axis_size(('req', 'mlp'))), ('req...  319 us
    reduce_scatter x1, waiting for transfers between devices, body(): lax.psum_scatter(mixed_all.astype(jnp.bfloat16), 'req', scatter_dimension...  73.7 us
    reduce_scatter x1, waiting for transfers between devices, body(): lax.psum_scatter(projected.astype(jnp.bfloat16), 'mlp', scatter_dimension...  31.4 us
    all_gather x1, waiting for transfers between devices, body(): next_normed = lax.all_gather(next_rows, 'mlp', axis=0, tiled=True)  25.5 us
    all_to_all x1, starting transfers between devices, body(): lax.all_to_all(blocks, 'mlp', split_axis=1, concat_axis=3, tiled=True)  16.8 us
    dot_general x1, matrix products, body(): upper = jnp.dot(piece, up_proj, preferred_element_type=jnp.float32)  13.8 us
  transfers between devices with their start and end apart: 7, of which 5 were waited for; matrix products, arithmetic and copies ran while one was open for 8% of the time, Pallas kernels for 0%

profile of v1, /device:TPU:1, one launch (start us, length us, event | category | flops | bytes accessed | tf_op | source)
XLA Modules:
  0.0 587.2 jit_solution(14922693148626995798)
XLA Ops:
  7.2 0.9 copy.70
  9.5 3.6 gather_fusion.1
  13.1 8.6 %all-to-all-start = ((bf16[16,1,64,2,128]{4,3,2,1,0:T(2,128)(2,1)}), bf16[16,1,64,2,128]{4,3,2,1,0:T(2,128)(2,1)S(1)}, u32[]{:S(2)}, u32[]{:S(2)}) async-start(bf16[16,1,64,2,128]{4,3,2,1,0:T(2,128)(2,1)} %bitcast.9), calls=%async_computation | async-start | bytes 1048576 | tf_op jit(solution)/shard_map/all_to_all | solution.py:87
  21.8 0.8 constant_dynamic-slice_fusion.1
  22.7 0.8 select_reduce_fusion.1
  24.9 1.7 or_and_fusion
  26.8 3.4 gather_fusion
  30.4 0.8 copy.77
  31.3 0.9 pad_add_fusion
  32.2 2.1 gather_fusion.2
  35.3 0.8 fusion
  36.1 1.0 fusion.1
  37.2 1.3 fusion.15
  38.5 1.0 slice-done.1
  39.5 2.3 convolution_convert_fusion.1
  41.8 31.4 %reduce-scatter.3.cloned.1.call-done = bf16[16,5120]{1,0:T(8,128)(2,1)} async-done(((bf16[128,5120]{1,0:T(8,128)(2,1)}), bf16[16,5120]{1,0:T(8,128)(2,1)}) %reduce-scatter.3.cloned.1.call-update) | async-done | bytes 163856 | tf_op jit(solution)/shard_map/reduce_scatter | solution.py:137
  73.3 1.2 fusion.26
  74.5 7.6 %stack.2 = bf16[128,16,5120]{2,1,0:T(8,128)(2,1)} broadcast(bf16[16,5120]{1,0:T(8,128)(2,1)S(1)} %fusion.28), dimensions={1,2} | broadcast | bytes 21135360 | tf_op jit(solution)/shard_map/stack | solution.py:144
  82.1 10.3 %all-to-all-start.1 = ((bf16[128,16,5120]{2,1,0:T(8,128)(2,1)}), bf16[128,16,5120]{2,1,0:T(8,128)(2,1)}, u32[]{:S(2)}, u32[]{:S(2)}) async-start(bf16[128,16,5120]{2,1,0:T(8,128)(2,1)} %stack.2), calls=%async_computation.2 | async-start | bytes 41943040 | tf_op jit(solution)/shard_map/all_to_all | solution.py:144
  93.2 319.1 %all-to-all-done.1 = bf16[128,16,5120]{2,1,0:T(8,128)(2,1)} async-done(((bf16[128,16,5120]{2,1,0:T(8,128)(2,1)}), bf16[128,16,5120]{2,1,0:T(8,128)(2,1)}, u32[]{:S(2)}, u32[]{:S(2)}) %all-to-all-start.1) | async-done | bytes 20971552 | tf_op jit(solution)/shard_map/all_to_all | solution.py:144
  412.3 11.1 %fusion.46 = f32[2048,108]{0,1:T(8,128)S(1)} fusion(bf16[2048,5120]{1,0:T(8,128)(2,1)} %bitcast.30, bf16[5120,108]{0,1:T(8,128)(2,1)S(1)} %copy-done), kind=kOutput, calls=%fused_computation.86 | convolution fusion | flops 2264924160 | bytes 22962176 | tf_op jit(solution)/shard_map/dot_general | solution.py:147
  423.4 13.8 %fusion.3 = bf16[2048,108]{0,1:T(8,128)(2,1)S(1)} fusion(bf16[2048,5120]{1,0:T(8,128)(2,1)} %bitcast.30, bf16[5120,108]{0,1:T(8,128)(2,1)S(1)} %copy-done.9, f32[2048,108]{0,1:T(8,128)S(1)} %fusion.46), kind=kOutput, calls=%fused_computation.11 | convolution fusion | flops 2266251264 | bytes 23404544 | tf_op jit(solution)/shard_map/dot_general | solution.py:148
  437.5 0.9 copy.82
  438.3 16.8 %all-to-all-start.2 = ((bf16[16,8,16,108]{3,2,0,1:T(8,128)(2,1)}), bf16[16,8,16,108]{3,2,0,1:T(8,128)(2,1)S(1)}, u32[]{:S(2)}, u32[]{:S(2)}) async-start(bf16[16,8,16,108]{3,2,0,1:T(8,128)(2,1)} %copy.82), calls=%async_computation.3 | async-start | bytes 1048576 | tf_op jit(solution)/shard_map/all_to_all | solution.py:151
  455.2 8.0 %reshape.285 = bf16[864,5120]{1,0:T(8,128)(2,1)} reshape(bf16[8,108,5120]{2,1,0:T(8,128)(2,1)} %all-gather.6.cloned.1.call-done) | data formatting | bytes 17694720
  463.1 1.5 all-to-all-done.2
  465.5 7.7 %convolution_convert_fusion = bf16[256,5120]{1,0:T(8,128)(2,1)} fusion(bf16[256,864]{1,0:T(8,128)(2,1)S(1)} %reshape.259, bf16[864,5120]{1,0:T(8,128)(2,1)} %reshape.285), kind=kOutput, calls=%fused_computation.3 | convolution fusion | flops 2266234880 | bytes 11911168 | tf_op jit(solution)/shard_map/dot_general | solution.py:153
  473.2 73.7 %reduce-scatter.5.cloned.1.call-done = bf16[16,5120]{1,0:T(8,128)(2,1)} async-done(((bf16[256,5120]{1,0:T(8,128)(2,1)}), bf16[16,5120]{1,0:T(8,128)(2,1)}) %reduce-scatter.5.cloned.1.call-update) | async-done | bytes 163856 | tf_op jit(solution)/shard_map/reduce_scatter | solution.py:158
  546.9 1.1 fusion.23
  548.1 0.8 fusion.25
  548.9 25.5 %all-gather.4.cloned.1.call-done = bf16[128,5120]{1,0:T(8,128)(2,1)} async-done(((bf16[16,5120]{1,0:T(8,128)(2,1)}), bf16[128,5120]{1,0:T(8,128)(2,1)}) %all-gather.4.cloned.1.call-update) | async-done | bytes 1310736 | tf_op jit(solution)/shard_map/all_gather | solution.py:163
  574.3 6.3 %fusion.8 = bf16[128,896]{1,0:T(8,128)(2,1)} fusion(bf16[128,5120]{1,0:T(8,128)(2,1)} %all-gather.4.cloned.1.call-done, bf16[5120,896]{1,0:T(8,128)(2,1)} %param.36, f32[896]{0:T(1024)S(1)} %copy-done.7), kind=kOutput, calls=%fused_computation.16 | convolution fusion | flops 1174634496 | bytes 10718720 | tf_op jit(solution)/shard_map/dot_general | solution.py:165
  (70 shorter events, 6.4 us)
Async XLA Ops:
  7.2 405.1 %copy-start = (bf16[5120,108]{0,1:T(8,128)(2,1)S(1)}, bf16[5120,108]{0,1:T(8,128)(2,1)}, u32[]{:S(2)}) copy-start(bf16[5120,108]{0,1:T(8,128)(2,1)} %param.32) | copy-start | bytes 3317764
  7.2 24.0 %copy-start.8 = (s32[128]{0:T(128)S(1)}, s32[128]{0:T(128)}, u32[]{:S(2)}) copy-start(s32[128]{0:T(128)} %param.25) | copy-start | bytes 1540
  7.2 23.2 %copy-start.3 = (bf16[128,640]{1,0:T(8,128)(2,1)S(1)}, bf16[128,640]{1,0:T(8,128)(2,1)}, u32[]{:S(2)}) copy-start(bf16[128,640]{1,0:T(8,128)(2,1)} %param.19) | copy-start | bytes 491524
  13.1 19.2 %all-to-all-start = ((bf16[16,1,64,2,128]{4,3,2,1,0:T(2,128)(2,1)}), bf16[16,1,64,2,128]{4,3,2,1,0:T(2,128)(2,1)S(1)}, u32[]{:S(2)}, u32[]{:S(2)}) async-start(bf16[16,1,64,2,128]{4,3,2,1,0:T(2,128)(2,1)} %bitcast.9), calls=%async_computation | async-start | bytes 1048576 | tf_op jit(solution)/shard_map/all_to_all | solution.py:87
  21.7 51.6 %reduce-scatter.3.cloned.1.call-start = ((), (), s32[]{:S(2)}) async-start(), calls=%async_computation.5 | async-start | bytes 1474560 | tf_op jit(solution)/shard_map/reduce_scatter | solution.py:137
  30.4 4.6 copy-start.10
  34.4 0.9 copy-start.4
  35.3 1.9 copy-start.11
  36.1 2.4 slice-start
  37.2 2.3 slice-start.1
  39.5 34.9 %copy-start.5 = (f32[5120]{0:T(1024)S(1)}, f32[5120]{0:T(1024)}, u32[]{:S(2)}) copy-start(f32[5120]{0:T(1024)} %param.31) | copy-start | bytes 61444
  82.1 330.2 %all-to-all-start.1 = ((bf16[128,16,5120]{2,1,0:T(8,128)(2,1)}), bf16[128,16,5120]{2,1,0:T(8,128)(2,1)}, u32[]{:S(2)}, u32[]{:S(2)}) async-start(bf16[128,16,5120]{2,1,0:T(8,128)(2,1)} %stack.2), calls=%async_computation.2 | async-start | bytes 41943040 | tf_op jit(solution)/shard_map/all_to_all | solution.py:144
  92.4 362.7 %all-gather.6.cloned.1.call-start = ((), (), s32[]{:S(2)}) async-start(), calls=%async_computation.8 | async-start | bytes 10321920 | tf_op jit(solution)/shard_map/all_gather | solution.py:155
  412.3 11.1 %copy-start.9 = (bf16[5120,108]{0,1:T(8,128)(2,1)S(1)}, bf16[5120,108]{0,1:T(8,128)(2,1)}, u32[]{:S(2)}) copy-start(bf16[5120,108]{0,1:T(8,128)(2,1)} %param.33) | copy-start | bytes 3317764
  438.3 26.3 %all-to-all-start.2 = ((bf16[16,8,16,108]{3,2,0,1:T(8,128)(2,1)}), bf16[16,8,16,108]{3,2,0,1:T(8,128)(2,1)S(1)}, u32[]{:S(2)}, u32[]{:S(2)}) async-start(bf16[16,8,16,108]{3,2,0,1:T(8,128)(2,1)} %copy.82), calls=%async_computation.3 | async-start | bytes 1048576 | tf_op jit(solution)/shard_map/all_to_all | solution.py:151
  455.2 91.8 %reduce-scatter.5.cloned.1.call-start = ((), (), s32[]{:S(2)}) async-start(), calls=%async_computation.6 | async-start | bytes 2785280 | tf_op jit(solution)/shard_map/reduce_scatter | solution.py:158
  465.4 82.6 %copy-start.6 = (f32[5120]{0:T(1024)S(1)}, f32[5120]{0:T(1024)}, u32[]{:S(2)}) copy-start(f32[5120]{0:T(1024)} %param.35) | copy-start | bytes 61444
  465.5 108.9 %copy-start.7 = (f32[896]{0:T(1024)S(1)}, f32[896]{0:T(1024)}, u32[]{:S(2)}) copy-start(f32[896]{0:T(1024)} %param.37) | copy-start | bytes 10756
  473.2 101.1 %all-gather.4.cloned.1.call-start = ((), (), s32[]{:S(2)}) async-start(), calls=%async_computation.7 | async-start | bytes 1474560 | tf_op jit(solution)/shard_map/all_gather | solution.py:163
  548.0 32.6 %copy-start.2 = (bf16[16,5120]{1,0:T(8,128)(2,1)}, bf16[16,5120]{1,0:T(8,128)(2,1)S(1)}, u32[]{:S(2)}) copy-start(bf16[16,5120]{1,0:T(8,128)(2,1)S(1)} %get-tuple-element.3) | copy-start | bytes 491524
  574.3 6.3 %copy-start.1 = (bf16[5120,108]{0,1:T(8,128)(2,1)S(1)}, bf16[5120,108]{0,1:T(8,128)(2,1)}, u32[]{:S(2)}) copy-start(bf16[5120,108]{0,1:T(8,128)(2,1)} %param.32) | copy-start | bytes 3317764
Sparse Core Ops, SparseCore 0:
  42.0 31.2 reduce-scatter.2
  95.0 123.4 all-gather.5
  473.3 73.6 reduce-scatter.4
  549.1 25.2 all-gather.3
